TPU v7x, 32 devices: a whole 2x2x4 slice. The times are simulated.
32 devices in a mesh: groups: 2 (over y), sky: 16 (over z, x, core).
Axes of the slice: x: 2, y: 2, z: 4, core: 2. Of those that a mesh axis runs over, the one named last changes fastest.
Arguments:
- model: float32 [64, 6, 256, 128], P(('groups', 'sky')), parts along dimension 0, may hold values from 0 to 2
- exposures: bfloat16 [4096, 16, 128], P(('groups', 'sky')), parts along dimension 0, may hold values from -6 to 6
- inv_var: float32 [4096], P(('groups', 'sky')), parts along dimension 0, may hold values from 0.5 to 2
- step_size: float32 [6], replicated, may hold values from 0.2 to 0.6
- psf_taps: float32 [64, 56], P(('groups', 'sky')), parts along dimension 0, may hold values from 0.05 to 1
- exp_batch: int32 [4096], P(('groups', 'sky')), parts along dimension 0, may hold values from 0 to 31
- send_plane: int32 [512, 16], P(('groups', 'sky')), parts along dimension 0, may hold values from -1 to 11, as said below
- send_row: int32 [512, 16], P(('groups', 'sky')), parts along dimension 0, may hold values from 0 to 248, as said below
- send_cover: int32 [512, 16], P(('groups', 'sky')), parts along dimension 0, may hold values from 0 to 16, as said below
- use_slot: int32 [4096, 2], P(('groups', 'sky')), parts along dimension 0, may hold values from -1 to 255, as said below
- use_start: int32 [4096, 2], P(('groups', 'sky')), parts along dimension 0, may hold values from 0 to 8, as said below
- use_stop: int32 [4096, 2], P(('groups', 'sky')), parts along dimension 0, may hold values from 0 to 16
- foot_lo: int32 [64], P(('groups', 'sky')), parts along dimension 0, may hold values from 0 to 63
- foot_hi: int32 [64], P(('groups', 'sky')), parts along dimension 0, may hold values from 193 to 256
Outputs:
- updated_model: float32 [64, 6, 256, 128], P(('groups', 'sky')), parts along dimension 0
- residual: float32 [4096, 16, 128], P(('groups', 'sky')), parts along dimension 0
There are 2 independent parts, one for each index of `groups`. A program takes and returns all parts, laid end to end along the dimension named above; an argument that names none is the same for every part. Nothing has to cross between parts.
Inputs may be any that keep to these rules, and one draw needn't show every extreme that they name: In each row of send_plane the covered rows of the live slots (send_cover) sum to at most 128, and on every device some row reaches it. A live slot of exposure owner d is used by exactly one intersection of one exposure on d, and every intersection with use_slot >= 0 names a live slot; all pieces of an exposure come from planes of one band. `send_row`: for a live slot, the tile rows that its piece covers lie inside the tile. send_cover of a live slot equals use_stop - use_start of the intersection that uses it. `use_slot`: each exposure has 1 to 2 live intersections, first in order; -1 after them. `use_start`: the live intersections of an exposure cover rows 0 to 15 in order without gaps; dead ones have start and stop 0.
All inputs are finite; a program needn't handle non-finite values.
Results may differ from a plain program's by a relative error of at most 0.0011.
Values may be sent and summed in bfloat16 or wider, within the bound.
A program may use at most 128 MiB of HBM per device.

v0:
```python
import functools

import jax
import jax.numpy as jnp
from jax import lax
from jax.experimental import pallas as pl
from jax.experimental.pallas import tpu as pltpu
from jax.sharding import PartitionSpec as P

NPSF = 4
TAPS = 7
ITERS = 2
LEAD = 8
F32 = jnp.float32
BF16 = jnp.bfloat16


def vmem():
    return pl.BlockSpec(memory_space=pltpu.VMEM)


def smem():
    return pl.BlockSpec(memory_space=pltpu.SMEM)


def pack_rows(image, packed, plane, row, cover, rows_each, tile_rows, height):
    peers, capacity = plane.shape

    def one_peer(o, carry):
        offset = o * rows_each
        for c in range(capacity):
            source = jnp.maximum(plane[o, c], 0) * tile_rows + row[o, c]
            packed[pl.ds(offset, height), :] = image[pl.ds(source, height), :]
            offset = offset + cover[o, c]
        return carry

    lax.fori_loop(0, peers, one_peer, 0)


def emit_packed(packed, out, rows_each):
    def one_peer(o, carry):
        start = pl.multiple_of(o * rows_each, 16)
        out[o, pl.ds(0, rows_each), :] = packed[pl.ds(start, rows_each), :].astype(BF16)
        return carry

    lax.fori_loop(0, out.shape[0], one_peer, 0)


def first_kernel(rows_each, tile_rows, height, plane, row, cover, model, banks, out, image, packed):
    total = model.shape[0]
    image[pl.ds(0, total), :] = model[...]
    image[pl.ds(total, height), :] = jnp.zeros((height, model.shape[1]), F32)
    pack_rows(image, packed, plane, row, cover, rows_each, tile_rows, height)
    emit_packed(packed, out, rows_each)
    extra = banks.shape[0]

    def add_banks(o, carry):
        out[o, pl.ds(rows_each, extra), :] = banks[...]
        return carry

    lax.fori_loop(0, out.shape[0], add_banks, 0)


def tile_kernel(rows_each, tile_rows, height, band_count, last, plane, row, cover, lo, hi, step, current,
                returned, *rest):
    if last:
        updated, grad, arrived = rest
    else:
        updated, out, grad, arrived, image, packed = rest
    total, columns = current.shape
    peers, capacity = plane.shape

    def clear(i, carry):
        start = pl.multiple_of(i * 64, 64)
        grad[pl.ds(start, 64), :] = jnp.zeros((64, columns), F32)
        return carry

    lax.fori_loop(0, total // 64, clear, 0)
    grad[pl.ds(total, height), :] = jnp.zeros((height, columns), F32)

    def widen(o, carry):
        start = pl.multiple_of(o * rows_each, 16)
        arrived[pl.ds(start, rows_each), :] = returned[o].astype(F32)
        return carry

    lax.fori_loop(0, peers, widen, 0)
    arrived[pl.ds(peers * rows_each, height), :] = jnp.zeros((height, columns), F32)
    position = lax.broadcasted_iota(jnp.int32, (height, columns), 0)

    def one_peer(o, carry):
        offset = o * rows_each
        for c in range(capacity):
            target = jnp.maximum(plane[o, c], 0) * tile_rows + row[o, c]
            count = cover[o, c]
            part = jnp.where(position < count, arrived[pl.ds(offset, height), :], 0.0)
            grad[pl.ds(target, height), :] += part
            offset = offset + count
        return carry

    lax.fori_loop(0, peers, one_peer, 0)
    tile_position = lax.broadcasted_iota(jnp.int32, (tile_rows, columns), 0)

    def one_plane(p, carry):
        tile = p // band_count
        start = pl.multiple_of(p * tile_rows, 8)
        here = pl.ds(start, tile_rows)
        moved = jnp.maximum(current[here, :] - step[p % band_count] * grad[here, :], 0.0)
        moved = jnp.where((tile_position >= lo[tile]) & (tile_position < hi[tile]), moved, 0.0)
        updated[here, :] = moved
        if not last:
            image[here, :] = moved
        return carry

    lax.fori_loop(0, total // tile_rows, one_plane, 0)
    if not last:
        image[pl.ds(total, height), :] = jnp.zeros((height, columns), F32)
        pack_rows(image, packed, plane, row, cover, rows_each, tile_rows, height)
        emit_packed(packed, out, rows_each)


def convolve(image, base, taps, taps_base, direction, masks):
    height, columns = masks[0].shape
    half = TAPS // 2
    rows = [image[pl.ds(base - direction * (u - half), height), :] for u in range(TAPS)]
    total = None
    for v in range(TAPS):
        part = None
        for u in range(TAPS):
            term = taps[pl.ds(taps_base + (u * TAPS + v), 1), :] * rows[u]
            part = term if part is None else part + term
        shift = direction * (v - half)
        if shift != 0:
            part = jnp.where(masks[shift + half], pltpu.roll(part, shift % columns, 1), 0.0)
        total = part if total is None else total + part
    return total


def exposure_kernel(rows_each, bank_rows, unroll, slot, start, stop, batch, weight, arrived, taps, observed,
                    residual, out, gathered, stamps, errors, length, begin, source):
    count, height, columns = observed.shape
    peers = out.shape[0]
    meets = slot.shape[1]
    slots = length.shape[0]
    capacity = slots // peers
    pitch = height + LEAD
    half = TAPS // 2

    def clear_slots(i, carry):
        length[i] = 0
        source[i] = LEAD
        return carry

    lax.fori_loop(0, slots, clear_slots, 0, unroll=8)

    def mark(e, carry):
        for k in range(meets):
            name = slot[e, k]

            @pl.when(name >= 0)
            def _():
                first = start[e, k]
                length[name] = stop[e, k] - first
                source[name] = e * pitch + LEAD + first
        return carry

    lax.fori_loop(0, count, mark, 0, unroll=4)

    def prefix(o, carry):
        offset = o * rows_each
        for c in range(capacity):
            begin[o * capacity + c] = offset
            offset = offset + length[o * capacity + c]
        return carry

    lax.fori_loop(0, peers, prefix, 0)

    gathered[pl.ds(0, height), :] = jnp.zeros((height, columns), F32)
    gathered[pl.ds(height + peers * rows_each, height), :] = jnp.zeros((height, columns), F32)

    def widen(o, carry):
        here = pl.multiple_of(o * rows_each + height, 8)
        gathered[pl.ds(here, rows_each), :] = arrived[o, pl.ds(0, rows_each), :].astype(F32)
        return carry

    lax.fori_loop(0, peers, widen, 0)
    gap = jnp.zeros((LEAD, columns), F32)
    stamps[pl.ds(0, LEAD), :] = gap
    errors[pl.ds(0, LEAD), :] = gap
    position = lax.broadcasted_iota(jnp.int32, (height, columns), 0)

    def assemble(e, carry):
        value = None
        for k in range(meets):
            name = slot[e, k]
            alive = name >= 0
            first = jnp.where(alive, start[e, k], height)
            at = height + jnp.where(alive, begin[jnp.maximum(name, 0)] - first, 0)
            piece = gathered[pl.ds(at, height), :]
            value = piece if value is None else jnp.where(position >= first, piece, value)
        here = pl.multiple_of(e * pitch + LEAD, 8)
        stamps[pl.ds(here, height), :] = value
        stamps[pl.ds(here + height, LEAD), :] = gap
        errors[pl.ds(here + height, LEAD), :] = gap
        return carry

    lax.fori_loop(0, count, assemble, 0, unroll=8)
    lane = lax.broadcasted_iota(jnp.int32, (height, columns), 1)
    masks = [
        (lane >= shift) if shift > 0 else (lane < columns + shift) for shift in range(-half, half + 1)
    ]

    def group(g, carry):
        which = [g * unroll + i for i in range(unroll)]
        for e in which:
            here = pl.multiple_of(e * pitch + LEAD, 8)
            predicted = convolve(stamps, here, taps, batch[e] * bank_rows, 1, masks)
            error = weight[e] * (predicted - observed[e].astype(F32))
            residual[e] = error
            errors[pl.ds(here, height), :] = error.astype(BF16).astype(F32)
        for e in which:
            here = pl.multiple_of(e * pitch + LEAD, 8)
            stamps[pl.ds(here, height), :] = convolve(errors, here, taps, batch[e] * bank_rows, -1, masks)
        return carry

    lax.fori_loop(0, count // unroll, group, 0)

    def give(o, carry):
        for c in range(capacity):
            name = o * capacity + c
            gathered[pl.ds(begin[name], height), :] = stamps[pl.ds(source[name], height), :]
        return carry

    lax.fori_loop(0, peers, give, 0)
    emit_packed(gathered, out, rows_each)


def body(model, exposures, inv_var, step_size, psf_taps, exp_batch, send_plane, send_row, send_cover, use_slot,
         use_start, use_stop, foot_lo, foot_hi):
    tile_count, band_count, tile_rows, columns = model.shape
    count, height, _ = exposures.shape
    peers, capacity = send_plane.shape
    rows_each = capacity * height // 2
    total = tile_count * band_count * tile_rows
    packed_rows = peers * rows_each
    own_banks, width = psf_taps.shape
    extra = -(-own_banks // 16) * 16
    bank_rows = -(-TAPS * TAPS // 8) * 8
    unroll = 4 if count % 4 == 0 else 1

    shaped = psf_taps.reshape(own_banks, 2 * NPSF, TAPS)
    shaped = shaped / jnp.sum(shaped, axis=-1, keepdims=True)
    banks = shaped.reshape(own_banks, width).astype(BF16)
    banks = jnp.pad(banks, ((0, extra - own_banks), (0, columns - width)))

    image_scratch = pltpu.VMEM((total + height, columns), F32)
    packed_scratch = pltpu.VMEM((packed_rows + height, columns), F32)
    exchange = functools.partial(lax.all_to_all, axis_name="sky", split_axis=0, concat_axis=0, tiled=True)

    current = model.reshape(total, columns)
    outbound = pl.pallas_call(
        functools.partial(first_kernel, rows_each, tile_rows, height),
        out_shape=jax.ShapeDtypeStruct((peers, rows_each + extra, columns), BF16),
        in_specs=[smem()] * 3 + [vmem()] * 2,
        out_specs=vmem(),
        scratch_shapes=[image_scratch, packed_scratch],
        name="first_pack",
    )(send_plane, send_row, send_cover, current, banks)
    residual = None
    taps = None
    for sweep in range(ITERS):
        arrived = exchange(outbound)
        if sweep == 0:
            pool = arrived[:, rows_each : rows_each + own_banks, :width].astype(F32)
            pool = pool.reshape(peers * own_banks, 2, NPSF, TAPS)
            kernels = jnp.sum(pool[:, 0, :, :, None] * pool[:, 1, :, None, :], axis=1) / NPSF
            kernels = kernels.reshape(peers * own_banks, TAPS * TAPS)
            kernels = jnp.pad(kernels, ((0, 0), (0, bank_rows - TAPS * TAPS)))
            taps = jnp.broadcast_to(
                kernels.reshape(peers * own_banks * bank_rows, 1), (peers * own_banks * bank_rows, columns)
            )
        residual, outgoing = pl.pallas_call(
            functools.partial(exposure_kernel, rows_each, bank_rows, unroll),
            out_shape=(
                jax.ShapeDtypeStruct(exposures.shape, F32),
                jax.ShapeDtypeStruct((peers, rows_each, columns), BF16),
            ),
            in_specs=[smem()] * 5 + [vmem()] * 3,
            out_specs=(vmem(), vmem()),
            scratch_shapes=[
                pltpu.VMEM((packed_rows + 2 * height, columns), F32),
                pltpu.VMEM((LEAD + count * (height + LEAD), columns), F32),
                pltpu.VMEM((LEAD + count * (height + LEAD), columns), F32),
                pltpu.SMEM((peers * capacity,), jnp.int32),
                pltpu.SMEM((peers * capacity,), jnp.int32),
                pltpu.SMEM((peers * capacity,), jnp.int32),
            ],
            name="exposures",
        )(use_slot, use_start, use_stop, exp_batch, inv_var, arrived, taps, exposures)
        returned = exchange(outgoing)
        last = sweep == ITERS - 1
        updated_shape = jax.ShapeDtypeStruct((total, columns), F32)
        outbound_shape = jax.ShapeDtypeStruct((peers, rows_each, columns), BF16)
        result = pl.pallas_call(
            functools.partial(tile_kernel, rows_each, tile_rows, height, band_count, last),
            out_shape=updated_shape if last else (updated_shape, outbound_shape),
            in_specs=[smem()] * 6 + [vmem()] * 2,
            out_specs=vmem() if last else (vmem(), vmem()),
            scratch_shapes=[image_scratch, packed_scratch] + ([] if last else [image_scratch, packed_scratch]),
            name="tiles_last" if last else "tiles",
        )(send_plane, send_row, send_cover, foot_lo, foot_hi, step_size, current, returned)
        if last:
            current = result
        else:
            current, outbound = result
    return current.reshape(model.shape), residual


def solution(mesh):
    both = ("groups", "sky")
    return jax.shard_map(
        body,
        mesh=mesh,
        in_specs=(
            P(both, None, None, None),
            P(both, None, None),
            P(both),
            P(),
            P(both, None),
            P(both),
            P(both, None),
            P(both, None),
            P(both, None),
            P(both, None),
            P(both, None),
            P(both, None),
            P(both),
            P(both),
        ),
        out_specs=(P(both, None, None, None), P(both, None, None)),
        check_vma=False,
    )
```

profile of v0, /device:TPU:9, one launch (start us, length us, event | category | flops | bytes accessed | tf_op | source)
XLA Modules:
  0.0 137.2 jit_solution(8136646704918057872)
XLA Ops:
  0.6 0.8 reshape.31
  1.4 0.2 fusion
  1.5 0.1 div.20
  1.6 0.7 divide_convert_fusion
  2.3 0.6 pad.8.banks
  2.9 0.0 copy-start.1
  2.9 0.0 copy-start.2
  2.9 0.0 copy-start.3
  2.9 3.5 %first_pack.1 = bf16[16,144,128]{2,1,0:T(8,128)(2,1)} custom-call(s32[16,16]{1,0:T(8,128)} %plane.5, s32[16,16]{1,0:T(8,128)} %row.5, s32[16,16]{1,0:T(8,128)} %cover.5, f32[3072,128]{1,0:T(8,128)} %bitcast.9, bf16[16,128]{1,0:T(8,128)(2,1)} %pad.8.banks), custom_call_target="tpu_custom_call" | custom-call | tf_op jit(solution)/shard_map/first_pack/pallas_call | solution.py:260
  6.5 6.5 %all-to-all-start = ((bf16[16,144,128]{2,1,0:T(8,128)(2,1)}), bf16[16,144,128]{2,1,0:T(8,128)(2,1)S(1)}, u32[]{:S(2)}, u32[]{:S(2)}) async-start(bf16[16,144,128]{2,1,0:T(8,128)(2,1)} %first_pack.1), calls=%async_computation | async-start | bytes 1179648 | tf_op jit(solution)/shard_map/all_to_all | solution.py:271
  13.0 0.0 copy-done.1
  13.0 0.7 copy.38.slot
  13.8 0.0 copy-done.2
  13.8 0.7 copy.39.start
  14.5 0.0 copy-done.3
  14.5 0.7 copy.40.stop
  15.2 13.3 %all-to-all-done.arrived = bf16[16,144,128]{2,1,0:T(8,128)(2,1)S(1)} async-done(((bf16[16,144,128]{2,1,0:T(8,128)(2,1)}), bf16[16,144,128]{2,1,0:T(8,128)(2,1)S(1)}, u32[]{:S(2)}, u32[]{:S(2)}) %all-to-all-start) | async-done | bytes 589856 | tf_op jit(solution)/shard_map/all_to_all | solution.py:271
  28.6 0.1 reshape.36
  28.8 0.1 copy.35
  28.8 0.1 copy.36
  28.9 0.1 multiply_reduce_fusion
  29.1 0.1 copy.44
  29.2 0.1 broadcast_in_dim.8
  29.2 1.2 broadcast_in_dim.9.taps
  30.5 0.0 copy-done
  30.5 20.2 %exposures.2 = (f32[128,16,128]{2,1,0:T(8,128)}, bf16[16,128,128]{2,1,0:T(8,128)(2,1)}) custom-call(s32[128,2]{1,0:T(8,128)} %copy.38.slot, s32[128,2]{1,0:T(8,128)} %copy.39.start, s32[128,2]{1,0:T(8,128)} %copy.40.stop, s32[128]{0:T(128)} %batch.3, f32[128]{0:T(128)} %weight.3, bf16[16,144,128]{2,1,0:T(8,128)(2,1)} %copy-done, ...), custom_call_target="tpu_custom_call" | custom-call | tf_op jit(solution)/shard_map/exposures/pallas_call | solution.py:281
  50.7 18.5 %all_to_all.20.returned = bf16[16,128,128]{2,1,0:T(8,128)(2,1)} all-to-all(bf16[16,128,128]{2,1,0:T(8,128)(2,1)} %get-tuple-element.7), channel_id=1, replica_groups=mesh['groups'=2,'sky'=16] {'sky'}, dimensions={0} | all-to-all | bytes 1048576 | tf_op jit(solution)/shard_map/all_to_all | solution.py:299
  69.2 6.0 %tiles.1 = (f32[3072,128]{1,0:T(8,128)}, bf16[16,128,128]{2,1,0:T(8,128)(2,1)}) custom-call(s32[16,16]{1,0:T(8,128)} %plane.5, s32[16,16]{1,0:T(8,128)} %row.5, s32[16,16]{1,0:T(8,128)} %cover.5, s32[2]{0:T(128)} %lo.3, s32[2]{0:T(128)} %hi.3, f32[6]{0:T(128)} %step.3, f32[3072,128]{1,0:T(8,128)} %bitcast.10, bf16[16,128,128]{2,1,0:T(8,128)(2,1)} %all_to_all.20.returned), custom_call_target="tpu_custom_call" | custom-call | tf_op jit(solution)/shard_map/tiles/pallas_call | solution.py:303
  75.2 18.5 %all_to_all.21.arrived = bf16[16,128,128]{2,1,0:T(8,128)(2,1)} all-to-all(bf16[16,128,128]{2,1,0:T(8,128)(2,1)} %get-tuple-element.9), channel_id=1, replica_groups=mesh['groups'=2,'sky'=16] {'sky'}, dimensions={0} | all-to-all | bytes 1048576 | tf_op jit(solution)/shard_map/all_to_all | solution.py:271
  93.8 20.2 %exposures.3 = (f32[128,16,128]{2,1,0:T(8,128)}, bf16[16,128,128]{2,1,0:T(8,128)(2,1)}) custom-call(s32[128,2]{1,0:T(8,128)} %copy.38.slot, s32[128,2]{1,0:T(8,128)} %copy.39.start, s32[128,2]{1,0:T(8,128)} %copy.40.stop, s32[128]{0:T(128)} %batch.3, f32[128]{0:T(128)} %weight.3, bf16[16,128,128]{2,1,0:T(8,128)(2,1)} %all_to_all.21.arrived, ...), custom_call_target="tpu_custom_call" | custom-call | tf_op jit(solution)/shard_map/exposures/pallas_call | solution.py:281
  114.0 18.5 %all_to_all.22.returned = bf16[16,128,128]{2,1,0:T(8,128)(2,1)} all-to-all(bf16[16,128,128]{2,1,0:T(8,128)(2,1)} %get-tuple-element.10), channel_id=1, replica_groups=mesh['groups'=2,'sky'=16] {'sky'}, dimensions={0} | all-to-all | bytes 1048576 | tf_op jit(solution)/shard_map/all_to_all | solution.py:299
  132.5 4.7 %tiles_last.1 = f32[3072,128]{1,0:T(8,128)} custom-call(s32[16,16]{1,0:T(8,128)} %plane.5, s32[16,16]{1,0:T(8,128)} %row.5, s32[16,16]{1,0:T(8,128)} %cover.5, s32[2]{0:T(128)} %lo.3, s32[2]{0:T(128)} %hi.3, f32[6]{0:T(128)} %step.3, f32[3072,128]{1,0:T(8,128)} %get-tuple-element.8.current, bf16[16,128,128]{2,1,0:T(8,128)(2,1)} %all_to_all.22.returned), custom_call_target="tpu_custom_call" | custom-call | tf_op jit(solution)/shard_map/tiles_last/pallas_call | solution.py:303
  (6 shorter events, 0.1 us)
Async XLA Ops:
  2.9 10.1 %copy-start.1 = (s32[128,2]{0,1:T(2,128)S(1)}, s32[128,2]{0,1:T(2,128)}, u32[]{:S(2)}) copy-start(s32[128,2]{0,1:T(2,128)} %param.23) | copy-start | bytes 3076
  2.9 10.8 %copy-start.2 = (s32[128,2]{0,1:T(2,128)S(1)}, s32[128,2]{0,1:T(2,128)}, u32[]{:S(2)}) copy-start(s32[128,2]{0,1:T(2,128)} %param.24) | copy-start | bytes 3076
  2.9 11.6 %copy-start.3 = (s32[128,2]{0,1:T(2,128)S(1)}, s32[128,2]{0,1:T(2,128)}, u32[]{:S(2)}) copy-start(s32[128,2]{0,1:T(2,128)} %param.25) | copy-start | bytes 3076
  6.5 22.1 %all-to-all-start = ((bf16[16,144,128]{2,1,0:T(8,128)(2,1)}), bf16[16,144,128]{2,1,0:T(8,128)(2,1)S(1)}, u32[]{:S(2)}, u32[]{:S(2)}) async-start(bf16[16,144,128]{2,1,0:T(8,128)(2,1)} %first_pack.1), calls=%async_computation | async-start | bytes 1179648 | tf_op jit(solution)/shard_map/all_to_all | solution.py:271
  28.6 1.9 %copy-start = (bf16[16,144,128]{2,1,0:T(8,128)(2,1)}, bf16[16,144,128]{2,1,0:T(8,128)(2,1)S(1)}, u32[]{:S(2)}) copy-start(bf16[16,144,128]{2,1,0:T(8,128)(2,1)S(1)} %all-to-all-done.arrived) | copy-start | bytes 1769476
where the time goes:
time: 139 us; the launch traced here: 137 us
  blocking collectives  55.6 us (40%)
  Pallas kernels  54.7 us (39%)
  waiting for transfers between devices  13.3 us (10%)
  starting transfers between devices  6.55 us (5%)
  local copies, waits for them, and re-layouts  5.44 us (4%)
    pallas_call x2, Pallas kernels, body(): pl.pallas_call(functools.partial(exposure_kernel, rows_each, bank_rows, u...  40.4 us
    all_to_all x2, blocking collectives, body(): returned = exchange(outgoing)  37.1 us
    all_to_all x1, blocking collectives, body(): arrived = exchange(outbound)  18.5 us
    all_to_all x1, waiting for transfers between devices, body(): arrived = exchange(outbound)  13.3 us
    pallas_call x2, Pallas kernels, body(): pl.pallas_call(functools.partial(tile_kernel, rows_each, tile_rows, heigh...  10.8 us
    all_to_all x1, starting transfers between devices, body(): arrived = exchange(outbound)  6.55 us
    pallas_call x1, Pallas kernels, body(): pl.pallas_call(functools.partial(first_kernel, rows_each, tile_rows, heig...  3.54 us
  transfers between devices with their start and end apart: 1, of which 1 were waited for; matrix products, arithmetic and copies ran while one was open for 2% of the time, Pallas kernels for 0%

commit v1 on v0

--- a/solution.py
+++ b/solution.py
@@ -2,6 +2,7 @@
 
 import jax
 import jax.numpy as jnp
+import numpy as np
 from jax import lax
 from jax.experimental import pallas as pl
 from jax.experimental.pallas import tpu as pltpu
@@ -10,7 +11,6 @@
 NPSF = 4
 TAPS = 7
 ITERS = 2
-LEAD = 8
 F32 = jnp.float32
 BF16 = jnp.bfloat16
 
@@ -46,7 +46,9 @@
     lax.fori_loop(0, out.shape[0], one_peer, 0)
 
 
-def first_kernel(rows_each, tile_rows, height, plane, row, cover, model, banks, out, image, packed):
+def first_kernel(rows_each, tile_rows, height, plane, row, cover, slot, start, stop, model, banks, out, begin, source,
+                 image, packed, length):
+    slot_tables(rows_each, height, out.shape[0], slot, start, stop, begin, source, length)
     total = model.shape[0]
     image[pl.ds(0, total), :] = model[...]
     image[pl.ds(total, height), :] = jnp.zeros((height, model.shape[1]), F32)
@@ -118,64 +120,40 @@
         emit_packed(packed, out, rows_each)
 
 
-def convolve(image, base, taps, taps_base, direction, masks):
-    height, columns = masks[0].shape
+def spread(value, target, direction, masks):
+    height, columns = value.shape
     half = TAPS // 2
-    rows = [image[pl.ds(base - direction * (u - half), height), :] for u in range(TAPS)]
-    total = None
     for v in range(TAPS):
-        part = None
-        for u in range(TAPS):
-            term = taps[pl.ds(taps_base + (u * TAPS + v), 1), :] * rows[u]
-            part = term if part is None else part + term
         shift = direction * (v - half)
+        part = value
         if shift != 0:
-            part = jnp.where(masks[shift + half], pltpu.roll(part, shift % columns, 1), 0.0)
-        total = part if total is None else total + part
-    return total
-
-
-def exposure_kernel(rows_each, bank_rows, unroll, slot, start, stop, batch, weight, arrived, taps, observed,
-                    residual, out, gathered, stamps, errors, length, begin, source):
+            part = jnp.where(masks[shift + half], pltpu.roll(value, shift % columns, 1), 0.0)
+        target[pl.ds(v * height, height), :] = part.astype(BF16)
+
+
+def apply(operator, shifted):
+    both = jnp.dot(operator, shifted, preferred_element_type=F32)
+    height = both.shape[0] // 2
+    return both[:height] + both[height:]
+
+
+def exposure_kernel(rows_each, unroll, slot, start, batch, weight, begin, source, arrived, operators, observed,
+                    residual, out, gathered, stamps, forward, backward):
     count, height, columns = observed.shape
     peers = out.shape[0]
     meets = slot.shape[1]
-    slots = length.shape[0]
-    capacity = slots // peers
-    pitch = height + LEAD
+    capacity = begin.shape[0] // peers
     half = TAPS // 2
-
-    def clear_slots(i, carry):
-        length[i] = 0
-        source[i] = LEAD
-        return carry
-
-    lax.fori_loop(0, slots, clear_slots, 0, unroll=8)
-
-    def mark(e, carry):
-        for k in range(meets):
-            name = slot[e, k]
-
-            @pl.when(name >= 0)
-            def _():
-                first = start[e, k]
-                length[name] = stop[e, k] - first
-                source[name] = e * pitch + LEAD + first
-        return carry
-
-    lax.fori_loop(0, count, mark, 0, unroll=4)
-
-    def prefix(o, carry):
-        offset = o * rows_each
-        for c in range(capacity):
-            begin[o * capacity + c] = offset
-            offset = offset + length[o * capacity + c]
-        return carry
-
-    lax.fori_loop(0, peers, prefix, 0)
 
     gathered[pl.ds(0, height), :] = jnp.zeros((height, columns), F32)
     gathered[pl.ds(height + peers * rows_each, height), :] = jnp.zeros((height, columns), F32)
+    stamps[pl.ds(count * height, height), :] = jnp.zeros((height, columns), F32)
+    used = TAPS * height
+    spare = forward.shape[1] - used
+    if spare:
+        for i in range(unroll):
+            forward[i, pl.ds(used, spare), :] = jnp.zeros((spare, columns), BF16)
+            backward[i, pl.ds(used, spare), :] = jnp.zeros((spare, columns), BF16)
 
     def widen(o, carry):
         here = pl.multiple_of(o * rows_each + height, 8)
@@ -183,12 +161,13 @@
         return carry
 
     lax.fori_loop(0, peers, widen, 0)
-    gap = jnp.zeros((LEAD, columns), F32)
-    stamps[pl.ds(0, LEAD), :] = gap
-    errors[pl.ds(0, LEAD), :] = gap
     position = lax.broadcasted_iota(jnp.int32, (height, columns), 0)
-
-    def assemble(e, carry):
+    lane = lax.broadcasted_iota(jnp.int32, (height, columns), 1)
+    masks = [
+        (lane >= shift) if shift > 0 else (lane < columns + shift) for shift in range(-half, half + 1)
+    ]
+
+    def assemble(e):
         value = None
         for k in range(meets):
             name = slot[e, k]
@@ -197,29 +176,20 @@
             at = height + jnp.where(alive, begin[jnp.maximum(name, 0)] - first, 0)
             piece = gathered[pl.ds(at, height), :]
             value = piece if value is None else jnp.where(position >= first, piece, value)
-        here = pl.multiple_of(e * pitch + LEAD, 8)
-        stamps[pl.ds(here, height), :] = value
-        stamps[pl.ds(here + height, LEAD), :] = gap
-        errors[pl.ds(here + height, LEAD), :] = gap
-        return carry
-
-    lax.fori_loop(0, count, assemble, 0, unroll=8)
-    lane = lax.broadcasted_iota(jnp.int32, (height, columns), 1)
-    masks = [
-        (lane >= shift) if shift > 0 else (lane < columns + shift) for shift in range(-half, half + 1)
-    ]
+        return value
 
     def group(g, carry):
         which = [g * unroll + i for i in range(unroll)]
-        for e in which:
-            here = pl.multiple_of(e * pitch + LEAD, 8)
-            predicted = convolve(stamps, here, taps, batch[e] * bank_rows, 1, masks)
+        for i, e in enumerate(which):
+            spread(assemble(e), forward.at[i], 1, masks)
+        for i, e in enumerate(which):
+            predicted = apply(operators[batch[e], 0], forward[i])
             error = weight[e] * (predicted - observed[e].astype(F32))
             residual[e] = error
-            errors[pl.ds(here, height), :] = error.astype(BF16).astype(F32)
-        for e in which:
-            here = pl.multiple_of(e * pitch + LEAD, 8)
-            stamps[pl.ds(here, height), :] = convolve(errors, here, taps, batch[e] * bank_rows, -1, masks)
+            spread(error, backward.at[i], -1, masks)
+        for i, e in enumerate(which):
+            here = pl.multiple_of(e * height, 8)
+            stamps[pl.ds(here, height), :] = apply(operators[batch[e], 1], backward[i])
         return carry
 
     lax.fori_loop(0, count // unroll, group, 0)
@@ -232,6 +202,120 @@
 
     lax.fori_loop(0, peers, give, 0)
     emit_packed(gathered, out, rows_each)
+
+
+def slot_tables(rows_each, height, peers, slot, start, stop, begin, source, length):
+    count, meets = slot.shape
+    slots = begin.shape[0]
+    capacity = slots // peers
+
+    def clear_slots(i, carry):
+        length[i] = 0
+        source[i] = 0
+        return carry
+
+    lax.fori_loop(0, slots, clear_slots, 0, unroll=16)
+
+    def mark(e, carry):
+        for k in range(meets):
+            name = slot[e, k]
+            first = start[e, k]
+            alive = name >= 0
+            length[jnp.where(alive, name, slots)] = stop[e, k] - first
+            name = jnp.where(alive, name, e * 0)
+            source[name] = jnp.where(alive, e * height + first, source[name])
+        return carry
+
+    lax.fori_loop(0, count, mark, 0, unroll=8)
+
+    def prefix(o, carry):
+        offset = o * rows_each
+        for c in range(capacity):
+            begin[o * capacity + c] = offset
+            offset = offset + length[o * capacity + c]
+        return carry
+
+    lax.fori_loop(0, peers, prefix, 0)
+
+
+def partner(me, i, peers):
+    if peers & (peers - 1):
+        return lax.rem(me + i, peers)
+    other = me
+    bit = 1
+    while bit < peers:
+        if i & bit:
+            other = other + (1 - 2 * lax.rem(me // bit, 2)) * bit
+        bit *= 2
+    return other
+
+
+def exchange_kernel(outgoing, incoming, send_sems, recv_sems, own_sem):
+    me = lax.axis_index("sky")
+    peers = outgoing.shape[0]
+    order = [base + d for base in range(0, peers, 4) for d in (2, 0, 3, 1) if 0 < base + d < peers]
+    barrier = pltpu.get_barrier_semaphore()
+    for i in order:
+        pl.semaphore_signal(
+            barrier, inc=1, device_id={"sky": partner(me, i, peers)}, device_id_type=pl.DeviceIdType.MESH
+        )
+    pl.semaphore_wait(barrier, peers - 1)
+    copies = []
+    for i in order:
+        to = partner(me, i, peers)
+        copy = pltpu.make_async_remote_copy(
+            src_ref=outgoing.at[to],
+            dst_ref=incoming.at[me],
+            send_sem=send_sems.at[i],
+            recv_sem=recv_sems.at[i],
+            device_id={"sky": to},
+            device_id_type=pl.DeviceIdType.MESH,
+        )
+        copy.start()
+        copies.append(copy)
+    own = pltpu.make_async_copy(outgoing.at[me], incoming.at[me], own_sem)
+    own.start()
+    own.wait()
+    for copy in copies:
+        copy.wait()
+
+
+def exchange(outgoing, ident):
+    peers = outgoing.shape[0]
+    return pl.pallas_call(
+        exchange_kernel,
+        out_shape=jax.ShapeDtypeStruct(outgoing.shape, outgoing.dtype),
+        in_specs=[pl.BlockSpec(memory_space=pl.ANY)],
+        out_specs=pl.BlockSpec(memory_space=pl.ANY),
+        scratch_shapes=[
+            pltpu.SemaphoreType.DMA((peers,)),
+            pltpu.SemaphoreType.DMA((peers,)),
+            pltpu.SemaphoreType.DMA,
+        ],
+        compiler_params=pltpu.CompilerParams(collective_id=ident, has_side_effects=True),
+        name="exchange",
+    )(outgoing)
+
+
+def operator_pattern(height, depth):
+    half = TAPS // 2
+    pattern = np.zeros((TAPS * TAPS, 2, height, depth), np.float32)
+    for v in range(TAPS):
+        for a in range(height):
+            for s in range(height):
+                if abs(a - s) <= half:
+                    pattern[(a - s + half) * TAPS + v, 0, a, v * height + s] = 1.0
+                    pattern[(s - a + half) * TAPS + v, 1, a, v * height + s] = 1.0
+    return pattern.reshape(TAPS * TAPS, -1)
+
+
+def build_operators(pool, height, depth):
+    kernels = jnp.sum(pool[:, 0, :, :, None] * pool[:, 1, :, None, :], axis=1) / NPSF
+    kernels = kernels.reshape(pool.shape[0], TAPS * TAPS)
+    full = jnp.dot(kernels, operator_pattern(height, depth), precision=lax.Precision.HIGHEST)
+    full = full.reshape(pool.shape[0], 2, height, depth)
+    coarse = lax.reduce_precision(full, 8, 7)
+    return jnp.concatenate([coarse, full - coarse], axis=2).astype(BF16)
 
 
 def body(model, exposures, inv_var, step_size, psf_taps, exp_batch, send_plane, send_row, send_cover, use_slot,
@@ -244,8 +328,9 @@
     packed_rows = peers * rows_each
     own_banks, width = psf_taps.shape
     extra = -(-own_banks // 16) * 16
-    bank_rows = -(-TAPS * TAPS // 8) * 8
-    unroll = 4 if count % 4 == 0 else 1
+    slots = peers * capacity
+    depth = -(-TAPS * height // 128) * 128
+    unroll = 8 if count % 8 == 0 else 1
 
     shaped = psf_taps.reshape(own_banks, 2 * NPSF, TAPS)
     shaped = shaped / jnp.sum(shaped, axis=-1, keepdims=True)
@@ -254,49 +339,44 @@
 
     image_scratch = pltpu.VMEM((total + height, columns), F32)
     packed_scratch = pltpu.VMEM((packed_rows + height, columns), F32)
-    exchange = functools.partial(lax.all_to_all, axis_name="sky", split_axis=0, concat_axis=0, tiled=True)
 
     current = model.reshape(total, columns)
-    outbound = pl.pallas_call(
+    outbound, begin, source = pl.pallas_call(
         functools.partial(first_kernel, rows_each, tile_rows, height),
-        out_shape=jax.ShapeDtypeStruct((peers, rows_each + extra, columns), BF16),
-        in_specs=[smem()] * 3 + [vmem()] * 2,
-        out_specs=vmem(),
-        scratch_shapes=[image_scratch, packed_scratch],
+        out_shape=(
+            jax.ShapeDtypeStruct((peers, rows_each + extra, columns), BF16),
+            jax.ShapeDtypeStruct((slots,), jnp.int32),
+            jax.ShapeDtypeStruct((slots,), jnp.int32),
+        ),
+        in_specs=[smem()] * 6 + [vmem()] * 2,
+        out_specs=(vmem(), smem(), smem()),
+        scratch_shapes=[image_scratch, packed_scratch, pltpu.SMEM((slots + 1,), jnp.int32)],
         name="first_pack",
-    )(send_plane, send_row, send_cover, current, banks)
+    )(send_plane, send_row, send_cover, use_slot, use_start, use_stop, current, banks)
     residual = None
-    taps = None
+    operators = None
     for sweep in range(ITERS):
-        arrived = exchange(outbound)
+        arrived = exchange(outbound, 0 if sweep == 0 else 1)
         if sweep == 0:
             pool = arrived[:, rows_each : rows_each + own_banks, :width].astype(F32)
-            pool = pool.reshape(peers * own_banks, 2, NPSF, TAPS)
-            kernels = jnp.sum(pool[:, 0, :, :, None] * pool[:, 1, :, None, :], axis=1) / NPSF
-            kernels = kernels.reshape(peers * own_banks, TAPS * TAPS)
-            kernels = jnp.pad(kernels, ((0, 0), (0, bank_rows - TAPS * TAPS)))
-            taps = jnp.broadcast_to(
-                kernels.reshape(peers * own_banks * bank_rows, 1), (peers * own_banks * bank_rows, columns)
-            )
+            operators = build_operators(pool.reshape(peers * own_banks, 2, NPSF, TAPS), height, depth)
         residual, outgoing = pl.pallas_call(
-            functools.partial(exposure_kernel, rows_each, bank_rows, unroll),
+            functools.partial(exposure_kernel, rows_each, unroll),
             out_shape=(
                 jax.ShapeDtypeStruct(exposures.shape, F32),
                 jax.ShapeDtypeStruct((peers, rows_each, columns), BF16),
             ),
-            in_specs=[smem()] * 5 + [vmem()] * 3,
+            in_specs=[smem()] * 6 + [vmem()] * 3,
             out_specs=(vmem(), vmem()),
             scratch_shapes=[
                 pltpu.VMEM((packed_rows + 2 * height, columns), F32),
-                pltpu.VMEM((LEAD + count * (height + LEAD), columns), F32),
-                pltpu.VMEM((LEAD + count * (height + LEAD), columns), F32),
-                pltpu.SMEM((peers * capacity,), jnp.int32),
-                pltpu.SMEM((peers * capacity,), jnp.int32),
-                pltpu.SMEM((peers * capacity,), jnp.int32),
+                pltpu.VMEM(((count + 1) * height, columns), F32),
+                pltpu.VMEM((unroll, depth, columns), BF16),
+                pltpu.VMEM((unroll, depth, columns), BF16),
             ],
             name="exposures",
-        )(use_slot, use_start, use_stop, exp_batch, inv_var, arrived, taps, exposures)
-        returned = exchange(outgoing)
+        )(use_slot, use_start, exp_batch, inv_var, begin, source, arrived, operators, exposures)
+        returned = exchange(outgoing, 1)
         last = sweep == ITERS - 1
         updated_shape = jax.ShapeDtypeStruct((total, columns), F32)
         outbound_shape = jax.ShapeDtypeStruct((peers, rows_each, columns), BF16)

time: 139 us -> 120 us (0.86)
  blocking collectives: 55.6 us -> 0 us
  Pallas kernels: 54.7 us -> 109 us
  waiting for transfers between devices: 13.3 us -> 0 us
  starting transfers between devices: 6.55 us -> 0 us
  other arithmetic: 0.95 us -> 2.91 us
    all_to_all x3 -> x0, blocking collectives: 55.6 us -> none  [the longest x2 37.1 us: body(): returned = exchange(outgoing)]
    pallas_call x2 -> x6, Pallas kernels: 40.4 us -> 89.5 us  [the longest x4 63.1 us: exchange(): pl.pallas_call(exchange_kernel, out_shape=jax.ShapeDtypeStruct(outgoing.s...]
    all_to_all x1 -> x0, waiting for transfers between devices: 13.3 us -> none  [body(): arrived = exchange(outbound)]
    all_to_all x1 -> x0, starting transfers between devices: 6.55 us -> none  [body(): arrived = exchange(outbound)]
    pallas_call x1, Pallas kernels: 3.54 us -> 8.64 us  [body(): pl.pallas_call(functools.partial(first_kernel, rows_each, tile_rows, heig...]
    unnamed x12 -> x5, local copies, waits for them, and re-layouts: 2.3 us -> 4.21 us
  transfers between devices with their start and end apart: 1 -> 0, of which waited for: 1 -> 0; matrix products, arithmetic and copies ran while one was open for 2% -> 0% of each run, Pallas kernels for 0% -> 0%
where the time goes in v1:
time: 120 us; the launch traced here: 119 us
  Pallas kernels  109 us (91%)
  local copies, waits for them, and re-layouts  6.02 us (5%)
  other arithmetic  2.91 us (2%)
    pallas_call x4, Pallas kernels, exchange(): pl.pallas_call(exchange_kernel, out_shape=jax.ShapeDtypeStruct(outgoing.s...  63.1 us
    pallas_call x2, Pallas kernels, body(): pl.pallas_call(functools.partial(exposure_kernel, rows_each, unroll), out...  26.4 us
    pallas_call x2, Pallas kernels, body(): pl.pallas_call(functools.partial(tile_kernel, rows_each, tile_rows, heigh...  10.8 us
    pallas_call x1, Pallas kernels, body(): pl.pallas_call(functools.partial(first_kernel, rows_each, tile_rows, heig...  8.64 us
    unnamed x5, local copies, waits for them, and re-layouts  4.21 us

profile of v1, /device:TPU:9, one launch (start us, length us, event | category | flops | bytes accessed | tf_op | source)
XLA Modules:
  0.0 119.3 jit_solution(15986873993306640033)
XLA Ops:
  0.6 0.8 reshape.36
  1.4 0.2 fusion
  1.5 0.1 div.20
  1.6 0.7 divide_convert_fusion
  2.3 0.6 pad.4.banks
  2.9 1.4 %copy.44.slot = s32[128,2]{1,0:T(8,128)} copy(s32[128,2]{0,1:T(2,128)} %param.24) | data formatting | bytes 2048 | tf_op args[9]
  4.3 1.4 %copy.45.start = s32[128,2]{1,0:T(8,128)} copy(s32[128,2]{0,1:T(2,128)} %param.25) | data formatting | bytes 2048 | tf_op args[10]
  5.7 1.4 %copy.38.stop = s32[128,2]{1,0:T(8,128)} copy(s32[128,2]{0,1:T(2,128)} %param.26) | data formatting | bytes 2048 | tf_op args[11]
  7.1 0.0 copy-start
  7.1 8.6 %first_pack.1 = (bf16[16,144,128]{2,1,0:T(8,128)(2,1)}, s32[256]{0:T(256)}, s32[256]{0:T(256)}) custom-call(s32[16,16]{1,0:T(8,128)} %plane.5, s32[16,16]{1,0:T(8,128)} %row.5, s32[16,16]{1,0:T(8,128)} %cover.5, s32[128,2]{1,0:T(8,128)} %copy.44.slot, s32[128,2]{1,0:T(8,128)} %copy.45.start, s32[128,2]{1,0:T(8,128)} %copy.38.stop, f32[3072,128]{1,0:T(8,128)} %bitcast.13, ...), custom_call_target="tpu_custom_call" | custom-call | tf_op jit(solution)/shard_map/first_pack/pallas_call | solution.py:344
  15.8 18.4 %exchange.4.arrived = bf16[16,144,128]{2,1,0:T(8,128)(2,1)} custom-call(bf16[16,144,128]{2,1,0:T(8,128)(2,1)} %get-tuple-element.12.outgoing), custom_call_target="tpu_custom_call" | custom-call | tf_op jit(solution)/shard_map/exchange/pallas_call | solution.py:285
  34.2 0.8 slice_convert_fusion
  35.0 0.1 reshape.41
  35.2 0.1 copy.39
  35.3 0.1 copy.40
  35.4 0.1 multiply_reduce_fusion
  35.5 0.0 copy-done
  35.5 0.7 fusion.2
  36.2 0.3 reduce-precision_convert_fusion
  36.5 0.9 pad_maximum_fusion.operators
  37.4 13.2 %exposures.2 = (f32[128,16,128]{2,1,0:T(8,128)}, bf16[16,128,128]{2,1,0:T(8,128)(2,1)}) custom-call(s32[128,2]{1,0:T(8,128)} %copy.44.slot, s32[128,2]{1,0:T(8,128)} %copy.45.start, s32[128]{0:T(128)} %batch.3, f32[128]{0:T(128)} %weight.3, s32[256]{0:T(256)} %get-tuple-element.10.begin, s32[256]{0:T(256)} %get-tuple-element.11.source, ...), custom_call_target="tpu_custom_call" | custom-call | tf_op jit(solution)/shard_map/exposures/pallas_call | solution.py:363
  50.6 14.9 %exchange.5.returned = bf16[16,128,128]{2,1,0:T(8,128)(2,1)} custom-call(bf16[16,128,128]{2,1,0:T(8,128)(2,1)} %get-tuple-element.13.outgoing), custom_call_target="tpu_custom_call" | custom-call | tf_op jit(solution)/shard_map/exchange/pallas_call | solution.py:285
  65.5 6.0 %tiles.1 = (f32[3072,128]{1,0:T(8,128)}, bf16[16,128,128]{2,1,0:T(8,128)(2,1)}) custom-call(s32[16,16]{1,0:T(8,128)} %plane.5, s32[16,16]{1,0:T(8,128)} %row.5, s32[16,16]{1,0:T(8,128)} %cover.5, s32[2]{0:T(128)} %lo.3, s32[2]{0:T(128)} %hi.3, f32[6]{0:T(128)} %step.3, f32[3072,128]{1,0:T(8,128)} %bitcast.14, bf16[16,128,128]{2,1,0:T(8,128)(2,1)} %exchange.5.returned), custom_call_target="tpu_custom_call" | custom-call | tf_op jit(solution)/shard_map/tiles/pallas_call | solution.py:383
  71.6 14.9 %exchange.6.arrived = bf16[16,128,128]{2,1,0:T(8,128)(2,1)} custom-call(bf16[16,128,128]{2,1,0:T(8,128)(2,1)} %get-tuple-element.15.outgoing), custom_call_target="tpu_custom_call" | custom-call | tf_op jit(solution)/shard_map/exchange/pallas_call | solution.py:285
  86.5 13.2 %exposures.3 = (f32[128,16,128]{2,1,0:T(8,128)}, bf16[16,128,128]{2,1,0:T(8,128)(2,1)}) custom-call(s32[128,2]{1,0:T(8,128)} %copy.44.slot, s32[128,2]{1,0:T(8,128)} %copy.45.start, s32[128]{0:T(128)} %batch.3, f32[128]{0:T(128)} %weight.3, s32[256]{0:T(256)} %get-tuple-element.10.begin, s32[256]{0:T(256)} %get-tuple-element.11.source, ...), custom_call_target="tpu_custom_call" | custom-call | tf_op jit(solution)/shard_map/exposures/pallas_call | solution.py:363
  99.7 14.9 %exchange.7.returned = bf16[16,128,128]{2,1,0:T(8,128)(2,1)} custom-call(bf16[16,128,128]{2,1,0:T(8,128)(2,1)} %get-tuple-element.16.outgoing), custom_call_target="tpu_custom_call" | custom-call | tf_op jit(solution)/shard_map/exchange/pallas_call | solution.py:285
  114.6 4.7 %tiles_last.1 = f32[3072,128]{1,0:T(8,128)} custom-call(s32[16,16]{1,0:T(8,128)} %plane.5, s32[16,16]{1,0:T(8,128)} %row.5, s32[16,16]{1,0:T(8,128)} %cover.5, s32[2]{0:T(128)} %lo.3, s32[2]{0:T(128)} %hi.3, f32[6]{0:T(128)} %step.3, f32[3072,128]{1,0:T(8,128)} %get-tuple-element.14.current, bf16[16,128,128]{2,1,0:T(8,128)(2,1)} %exchange.7.returned), custom_call_target="tpu_custom_call" | custom-call | tf_op jit(solution)/shard_map/tiles_last/pallas_call | solution.py:383
  (3 shorter events, 0.0 us)
Async XLA Ops:
  7.1 28.3 %copy-start = (f32[2,16,128,49]{2,3,1,0:T(8,128)S(1)}, f32[2,16,128,49]{2,3,1,0:T(8,128)}, u32[]{:S(2)}) copy-start(f32[2,16,128,49]{2,3,1,0:T(8,128)} %constant.21) | copy-start | bytes 2408452

commit v2 on v1

--- a/solution.py
+++ b/solution.py
@@ -46,9 +46,7 @@
     lax.fori_loop(0, out.shape[0], one_peer, 0)
 
 
-def first_kernel(rows_each, tile_rows, height, plane, row, cover, slot, start, stop, model, banks, out, begin, source,
-                 image, packed, length):
-    slot_tables(rows_each, height, out.shape[0], slot, start, stop, begin, source, length)
+def first_kernel(rows_each, tile_rows, height, plane, row, cover, model, banks, out, image, packed):
     total = model.shape[0]
     image[pl.ds(0, total), :] = model[...]
     image[pl.ds(total, height), :] = jnp.zeros((height, model.shape[1]), F32)
@@ -131,17 +129,22 @@
         target[pl.ds(v * height, height), :] = part.astype(BF16)
 
 
-def apply(operator, shifted):
+def apply(operators, bank, way, shifted):
+    operator = jnp.concatenate([operators[bank, 0, way], operators[bank, 1, way]], axis=0)
     both = jnp.dot(operator, shifted, preferred_element_type=F32)
     height = both.shape[0] // 2
     return both[:height] + both[height:]
 
 
-def exposure_kernel(rows_each, unroll, slot, start, batch, weight, begin, source, arrived, operators, observed,
-                    residual, out, gathered, stamps, forward, backward):
+def exposure_kernel(rows_each, unroll, last, at, first, batch, weight, begin, source, arrived, operators, observed,
+                    *rest):
+    if last:
+        residual, out, gathered, stamps, forward, backward = rest
+    else:
+        out, gathered, stamps, forward, backward = rest
     count, height, columns = observed.shape
     peers = out.shape[0]
-    meets = slot.shape[1]
+    meets = at.shape[0]
     capacity = begin.shape[0] // peers
     half = TAPS // 2
 
@@ -170,12 +173,8 @@
     def assemble(e):
         value = None
         for k in range(meets):
-            name = slot[e, k]
-            alive = name >= 0
-            first = jnp.where(alive, start[e, k], height)
-            at = height + jnp.where(alive, begin[jnp.maximum(name, 0)] - first, 0)
-            piece = gathered[pl.ds(at, height), :]
-            value = piece if value is None else jnp.where(position >= first, piece, value)
+            piece = gathered[pl.ds(at[k, e], height), :]
+            value = piece if value is None else jnp.where(position >= first[k, e], piece, value)
         return value
 
     def group(g, carry):
@@ -183,13 +182,14 @@
         for i, e in enumerate(which):
             spread(assemble(e), forward.at[i], 1, masks)
         for i, e in enumerate(which):
-            predicted = apply(operators[batch[e], 0], forward[i])
+            predicted = apply(operators, batch[e], 0, forward[i])
             error = weight[e] * (predicted - observed[e].astype(F32))
-            residual[e] = error
+            if last:
+                residual[e] = error
             spread(error, backward.at[i], -1, masks)
         for i, e in enumerate(which):
             here = pl.multiple_of(e * height, 8)
-            stamps[pl.ds(here, height), :] = apply(operators[batch[e], 1], backward[i])
+            stamps[pl.ds(here, height), :] = apply(operators, batch[e], 1, backward[i])
         return carry
 
     lax.fori_loop(0, count // unroll, group, 0)
@@ -204,38 +204,22 @@
     emit_packed(gathered, out, rows_each)
 
 
-def slot_tables(rows_each, height, peers, slot, start, stop, begin, source, length):
-    count, meets = slot.shape
-    slots = begin.shape[0]
-    capacity = slots // peers
-
-    def clear_slots(i, carry):
-        length[i] = 0
-        source[i] = 0
-        return carry
-
-    lax.fori_loop(0, slots, clear_slots, 0, unroll=16)
-
-    def mark(e, carry):
-        for k in range(meets):
-            name = slot[e, k]
-            first = start[e, k]
-            alive = name >= 0
-            length[jnp.where(alive, name, slots)] = stop[e, k] - first
-            name = jnp.where(alive, name, e * 0)
-            source[name] = jnp.where(alive, e * height + first, source[name])
-        return carry
-
-    lax.fori_loop(0, count, mark, 0, unroll=8)
-
-    def prefix(o, carry):
-        offset = o * rows_each
-        for c in range(capacity):
-            begin[o * capacity + c] = offset
-            offset = offset + length[o * capacity + c]
-        return carry
-
-    lax.fori_loop(0, peers, prefix, 0)
+def slot_tables(rows_each, height, peers, capacity, use_slot, use_start, use_stop):
+    slots = peers * capacity
+    names, start, stop = use_slot.T, use_start.T, use_stop.T
+    alive = names >= 0
+    first = jnp.where(alive, start, height)
+    flat = names.reshape(-1)
+    length = jnp.where(alive, stop - start, 0).reshape(-1)
+    every = jnp.concatenate([jnp.arange(slots, dtype=jnp.int32), flat])
+    peer = jnp.maximum(every, 0) // capacity
+    earlier = (flat[None, :] >= (peer * capacity)[:, None]) & (flat[None, :] < every[:, None])
+    begin = peer * rows_each + jnp.sum(jnp.where(earlier, length[None, :], 0), axis=1)
+    row = (jnp.arange(names.shape[1], dtype=jnp.int32) * height)[None, :] + start
+    same = flat[None, :] == jnp.arange(slots, dtype=jnp.int32)[:, None]
+    source = jnp.sum(jnp.where(same, row.reshape(1, -1), 0), axis=1)
+    at = height + jnp.where(alive, begin[slots:].reshape(names.shape) - first, 0)
+    return at, first, begin[:slots], source
 
 
 def partner(me, i, peers):
@@ -309,13 +293,20 @@
     return pattern.reshape(TAPS * TAPS, -1)
 
 
-def build_operators(pool, height, depth):
-    kernels = jnp.sum(pool[:, 0, :, :, None] * pool[:, 1, :, None, :], axis=1) / NPSF
-    kernels = kernels.reshape(pool.shape[0], TAPS * TAPS)
-    full = jnp.dot(kernels, operator_pattern(height, depth), precision=lax.Precision.HIGHEST)
-    full = full.reshape(pool.shape[0], 2, height, depth)
-    coarse = lax.reduce_precision(full, 8, 7)
-    return jnp.concatenate([coarse, full - coarse], axis=2).astype(BF16)
+def point_spread(psf_taps):
+    own_banks = psf_taps.shape[0]
+    taps = psf_taps.reshape(own_banks, 2, NPSF, TAPS)
+    taps = lax.reduce_precision(taps / jnp.sum(taps, axis=-1, keepdims=True), 8, 7)
+    kernels = jnp.sum(taps[:, 0, :, :, None] * taps[:, 1, :, None, :], axis=1) / NPSF
+    kernels = kernels.reshape(own_banks, TAPS * TAPS)
+    coarse = lax.reduce_precision(kernels, 8, 7)
+    return jnp.concatenate([coarse, kernels - coarse], axis=1).astype(BF16)
+
+
+def build_operators(halves, height, depth):
+    pattern = jnp.asarray(operator_pattern(height, depth), BF16)
+    full = jnp.dot(halves.reshape(-1, TAPS * TAPS), pattern, preferred_element_type=F32).astype(BF16)
+    return full.reshape(-1, 2, 2, height, depth)
 
 
 def body(model, exposures, inv_var, step_size, psf_taps, exp_batch, send_plane, send_row, send_cover, use_slot,
@@ -326,58 +317,56 @@
     rows_each = capacity * height // 2
     total = tile_count * band_count * tile_rows
     packed_rows = peers * rows_each
-    own_banks, width = psf_taps.shape
+    own_banks = psf_taps.shape[0]
     extra = -(-own_banks // 16) * 16
-    slots = peers * capacity
     depth = -(-TAPS * height // 128) * 128
-    unroll = 8 if count % 8 == 0 else 1
-
-    shaped = psf_taps.reshape(own_banks, 2 * NPSF, TAPS)
-    shaped = shaped / jnp.sum(shaped, axis=-1, keepdims=True)
-    banks = shaped.reshape(own_banks, width).astype(BF16)
+    unroll = 16 if count % 16 == 0 else 1
+
+    banks = point_spread(psf_taps)
+    width = banks.shape[1]
     banks = jnp.pad(banks, ((0, extra - own_banks), (0, columns - width)))
+    at, first, begin, source = slot_tables(rows_each, height, peers, capacity, use_slot, use_start, use_stop)
 
     image_scratch = pltpu.VMEM((total + height, columns), F32)
     packed_scratch = pltpu.VMEM((packed_rows + height, columns), F32)
 
     current = model.reshape(total, columns)
-    outbound, begin, source = pl.pallas_call(
+    outbound = pl.pallas_call(
         functools.partial(first_kernel, rows_each, tile_rows, height),
-        out_shape=(
-            jax.ShapeDtypeStruct((peers, rows_each + extra, columns), BF16),
-            jax.ShapeDtypeStruct((slots,), jnp.int32),
-            jax.ShapeDtypeStruct((slots,), jnp.int32),
-        ),
-        in_specs=[smem()] * 6 + [vmem()] * 2,
-        out_specs=(vmem(), smem(), smem()),
-        scratch_shapes=[image_scratch, packed_scratch, pltpu.SMEM((slots + 1,), jnp.int32)],
+        out_shape=jax.ShapeDtypeStruct((peers, rows_each + extra, columns), BF16),
+        in_specs=[smem()] * 3 + [vmem()] * 2,
+        out_specs=vmem(),
+        scratch_shapes=[image_scratch, packed_scratch],
         name="first_pack",
-    )(send_plane, send_row, send_cover, use_slot, use_start, use_stop, current, banks)
+    )(send_plane, send_row, send_cover, current, banks)
     residual = None
     operators = None
     for sweep in range(ITERS):
         arrived = exchange(outbound, 0 if sweep == 0 else 1)
         if sweep == 0:
-            pool = arrived[:, rows_each : rows_each + own_banks, :width].astype(F32)
-            operators = build_operators(pool.reshape(peers * own_banks, 2, NPSF, TAPS), height, depth)
-        residual, outgoing = pl.pallas_call(
-            functools.partial(exposure_kernel, rows_each, unroll),
-            out_shape=(
-                jax.ShapeDtypeStruct(exposures.shape, F32),
-                jax.ShapeDtypeStruct((peers, rows_each, columns), BF16),
-            ),
+            halves = arrived[:, rows_each : rows_each + own_banks, :width]
+            operators = build_operators(halves, height, depth)
+        last = sweep == ITERS - 1
+        residual_shape = jax.ShapeDtypeStruct(exposures.shape, F32)
+        outgoing_shape = jax.ShapeDtypeStruct((peers, rows_each, columns), BF16)
+        result = pl.pallas_call(
+            functools.partial(exposure_kernel, rows_each, unroll, last),
+            out_shape=(residual_shape, outgoing_shape) if last else outgoing_shape,
             in_specs=[smem()] * 6 + [vmem()] * 3,
-            out_specs=(vmem(), vmem()),
+            out_specs=(vmem(), vmem()) if last else vmem(),
             scratch_shapes=[
                 pltpu.VMEM((packed_rows + 2 * height, columns), F32),
                 pltpu.VMEM(((count + 1) * height, columns), F32),
                 pltpu.VMEM((unroll, depth, columns), BF16),
                 pltpu.VMEM((unroll, depth, columns), BF16),
             ],
-            name="exposures",
-        )(use_slot, use_start, exp_batch, inv_var, begin, source, arrived, operators, exposures)
+            name="exposures_last" if last else "exposures",
+        )(at, first, exp_batch, inv_var, begin, source, arrived, operators, exposures)
+        if last:
+            residual, outgoing = result
+        else:
+            outgoing = result
         returned = exchange(outgoing, 1)
-        last = sweep == ITERS - 1
         updated_shape = jax.ShapeDtypeStruct((total, columns), F32)
         outbound_shape = jax.ShapeDtypeStruct((peers, rows_each, columns), BF16)
         result = pl.pallas_call(

time: 120 us -> 105 us (0.88)
  Pallas kernels: 109 us -> 93.1 us
  other arithmetic: 2.91 us -> 7.3 us
  local copies, waits for them, and re-layouts: 6.02 us -> 3.29 us
    pallas_call x2, Pallas kernels: 26.4 us -> 15.8 us  [body(): pl.pallas_call(functools.partial(exposure_kernel, rows_each, unroll, last...]
    pallas_call x1, Pallas kernels: 8.64 us -> 3.56 us  [body(): pl.pallas_call(functools.partial(first_kernel, rows_each, tile_rows, heig...]
    unnamed x5 -> x3, local copies, waits for them, and re-layouts: 4.21 us -> 0.9 us
    reduce_sum x1 -> x3, other arithmetic: 0.09 us -> 2.44 us  [the longest x1 1.37 us: slot_tables(): source = jnp.sum(jnp.where(same, row.reshape(1, -1), 0), axis=1)]
    add x0 -> x2, other arithmetic: none -> 1.39 us  [slot_tables(): peer * rows_each + jnp.sum(jnp.where(earlier, length[None, :], 0), axis=1)]
    slice x0 -> x2, local copies, waits for them, and re-layouts: none -> 1.36 us  [the longest x1 0.77 us: body(): halves = arrived[:, rows_each:rows_each + own_banks, :width]]
    select_n x0 -> x1, other arithmetic: none -> 1.28 us  [slot_tables(): first = jnp.where(alive, start, height)]
where the time goes in v2:
time: 105 us
  Pallas kernels  93.1 us (89%)
  other arithmetic  7.3 us (7%)
  local copies, waits for them, and re-layouts  3.29 us (3%)
    pallas_call x4, Pallas kernels, exchange(): pl.pallas_call(exchange_kernel, out_shape=jax.ShapeDtypeStruct(outgoing.s...  63 us
    pallas_call x2, Pallas kernels, body(): pl.pallas_call(functools.partial(exposure_kernel, rows_each, unroll, last...  15.8 us
    pallas_call x2, Pallas kernels, body(): pl.pallas_call(functools.partial(tile_kernel, rows_each, tile_rows, heigh...  10.8 us
    pallas_call x1, Pallas kernels, body(): pl.pallas_call(functools.partial(first_kernel, rows_each, tile_rows, heig...  3.56 us

profile of v2, /device:TPU:9, one launch (start us, length us, event | category | flops | bytes accessed | tf_op | source)
XLA Modules:
  0.0 104.7 jit_solution(5988312748268884903)
XLA Ops:
  0.6 0.7 fusion.14
  1.4 0.7 broadcast_multiply_fusion.1
  2.1 1.0 select_reduce_fusion
  3.0 0.7 multiply_add_fusion
  3.7 0.6 slice.17.begin
  4.3 0.7 fusion.9
  5.0 1.3 %bitcast_select_fusion = (s32[2,128]{1,0:T(2,128)}, s32[2,128]{1,0:T(2,128)}, s32[256]{0:T(256)S(1)}) fusion(s32[128,2]{0,1:T(2,128)} %param.25, s32[128,2]{0,1:T(2,128)} %param.24, s32[4,128]{1,0:T(4,128)S(1)} %fusion.9, s32[128]{0:T(128)S(1)} %iota_multiply_fusion), kind=kLoop, calls=%fused_computation.36 | loop fusion | flops 1536 | bytes 6656 | tf_op jit(solution)/shard_map/jit(_where)/select_n | solution.py:211
  6.3 1.4 %select_reduce_fusion.1.source = s32[256]{0:T(256)} fusion(s32[256]{0:T(256)S(1)} %get-tuple-element.18, s32[256]{0:T(256)} %bitcast.52), kind=kLoop, calls=%fused_computation.3 | loop fusion | flops 196352 | bytes 3072 | tf_op jit(solution)/shard_map/reduce_sum | solution.py:220
  7.7 0.8 reshape.65
  8.4 0.1 divide_reduce-precision_fusion
  8.5 0.1 copy.17
  8.6 0.1 multiply_reduce_fusion
  8.8 0.1 div.36
  8.8 0.7 fusion.6.banks
  9.5 0.0 copy-start
  9.5 3.6 %first_pack.1.outgoing = bf16[16,144,128]{2,1,0:T(8,128)(2,1)} custom-call(s32[16,16]{1,0:T(8,128)} %plane.5, s32[16,16]{1,0:T(8,128)} %row.5, s32[16,16]{1,0:T(8,128)} %cover.5, f32[3072,128]{1,0:T(8,128)} %bitcast.43, bf16[16,128]{1,0:T(8,128)(2,1)} %fusion.6.banks), custom_call_target="tpu_custom_call" | custom-call | tf_op jit(solution)/shard_map/first_pack/pallas_call | solution.py:334
  13.1 18.3 %exchange.4.arrived = bf16[16,144,128]{2,1,0:T(8,128)(2,1)} custom-call(bf16[16,144,128]{2,1,0:T(8,128)(2,1)} %first_pack.1.outgoing), custom_call_target="tpu_custom_call" | custom-call | tf_op jit(solution)/shard_map/exchange/pallas_call | solution.py:269
  31.4 0.8 slice.20
  32.2 0.1 reshape.66
  32.3 0.0 copy-done
  32.3 0.3 fusion
  32.6 0.9 copy.18
  33.5 7.7 %exposures.1.outgoing = bf16[16,128,128]{2,1,0:T(8,128)(2,1)} custom-call(s32[2,128]{1,0:T(2,128)} %get-tuple-element.13.at, s32[2,128]{1,0:T(2,128)} %get-tuple-element.12.first, s32[128]{0:T(128)} %batch.3, f32[128]{0:T(128)} %weight.3, s32[256]{0:T(256)} %slice.17.begin, s32[256]{0:T(256)} %select_reduce_fusion.1.source, ...), custom_call_target="tpu_custom_call" | custom-call | tf_op jit(solution)/shard_map/exposures/pallas_call | solution.py:352
  41.2 14.9 %exchange.5.returned = bf16[16,128,128]{2,1,0:T(8,128)(2,1)} custom-call(bf16[16,128,128]{2,1,0:T(8,128)(2,1)} %exposures.1.outgoing), custom_call_target="tpu_custom_call" | custom-call | tf_op jit(solution)/shard_map/exchange/pallas_call | solution.py:269
  56.1 6.0 %tiles.1 = (f32[3072,128]{1,0:T(8,128)}, bf16[16,128,128]{2,1,0:T(8,128)(2,1)}) custom-call(s32[16,16]{1,0:T(8,128)} %plane.5, s32[16,16]{1,0:T(8,128)} %row.5, s32[16,16]{1,0:T(8,128)} %cover.5, s32[2]{0:T(128)} %lo.3, s32[2]{0:T(128)} %hi.3, f32[6]{0:T(128)} %step.3, f32[3072,128]{1,0:T(8,128)} %bitcast.44, bf16[16,128,128]{2,1,0:T(8,128)(2,1)} %exchange.5.returned), custom_call_target="tpu_custom_call" | custom-call | tf_op jit(solution)/shard_map/tiles/pallas_call | solution.py:372
  62.1 14.9 %exchange.6.arrived = bf16[16,128,128]{2,1,0:T(8,128)(2,1)} custom-call(bf16[16,128,128]{2,1,0:T(8,128)(2,1)} %get-tuple-element.7.outgoing), custom_call_target="tpu_custom_call" | custom-call | tf_op jit(solution)/shard_map/exchange/pallas_call | solution.py:269
  77.0 8.1 %exposures_last.1 = (f32[128,16,128]{2,1,0:T(8,128)}, bf16[16,128,128]{2,1,0:T(8,128)(2,1)}) custom-call(s32[2,128]{1,0:T(2,128)} %get-tuple-element.13.at, s32[2,128]{1,0:T(2,128)} %get-tuple-element.12.first, s32[128]{0:T(128)} %batch.3, f32[128]{0:T(128)} %weight.3, s32[256]{0:T(256)} %slice.17.begin, s32[256]{0:T(256)} %select_reduce_fusion.1.source, ...), custom_call_target="tpu_custom_call" | custom-call | tf_op jit(solution)/shard_map/exposures_last/pallas_call | solution.py:352
  85.1 14.9 %exchange.7.returned = bf16[16,128,128]{2,1,0:T(8,128)(2,1)} custom-call(bf16[16,128,128]{2,1,0:T(8,128)(2,1)} %get-tuple-element.8.outgoing), custom_call_target="tpu_custom_call" | custom-call | tf_op jit(solution)/shard_map/exchange/pallas_call | solution.py:269
  100.0 4.7 %tiles_last.1 = f32[3072,128]{1,0:T(8,128)} custom-call(s32[16,16]{1,0:T(8,128)} %plane.5, s32[16,16]{1,0:T(8,128)} %row.5, s32[16,16]{1,0:T(8,128)} %cover.5, s32[2]{0:T(128)} %lo.3, s32[2]{0:T(128)} %hi.3, f32[6]{0:T(128)} %step.3, f32[3072,128]{1,0:T(8,128)} %get-tuple-element.6.current, bf16[16,128,128]{2,1,0:T(8,128)(2,1)} %exchange.7.returned), custom_call_target="tpu_custom_call" | custom-call | tf_op jit(solution)/shard_map/tiles_last/pallas_call | solution.py:372
  (6 shorter events, 0.0 us)
Async XLA Ops:
  9.5 22.7 %copy-start = (bf16[49,4096]{1,0:T(8,128)(2,1)S(1)}, bf16[49,4096]{1,0:T(8,128)(2,1)}, u32[]{:S(2)}) copy-start(bf16[49,4096]{1,0:T(8,128)(2,1)} %constant.41.clone) | copy-start | bytes 1204228
